TPU v7x, 32 devices: a whole 2x2x4 slice. The times are simulated.
32 devices in a mesh: row: 8 (over z, core), col: 4 (over y, x).
Axes of the slice: x: 2, y: 2, z: 4, core: 2. Of those that a mesh axis runs over, the one named last changes fastest.
Arguments:
- pair_elems: bfloat16 [320, 12288], P('row', 'col'), may hold values from -0.59765625 to 0.59765625
- counts: int32 [8], replicated, may hold values from 1 to 40, 200 in all
- val_band: int32 [320], replicated, may hold values from 0 to 127
- cond_band: int32 [320], replicated, may hold values from 0 to 511
- val_energy: float32 [128], replicated, may hold values from -12 to -0.5
- cond_energy: float32 [512], replicated, may hold values from 0.5 to 12
- frequency: float32 [3], replicated, may hold values from 0.3 to 6
Outputs:
- chi: float32 [3, 12288, 12288], P(None, 'row', 'col')
Inputs may be any that keep to these rules, and one draw needn't show every extreme that they name: counts sum to 200, and the largest is 40.
All inputs are finite; a program needn't handle non-finite values.
Results may differ from a plain program's by a relative error of at most 0.0028.
Values may be sent and summed in bfloat16 or wider, within the bound.
A program may use at most 128 MiB of HBM per device.

v0:
```python
import functools
import math

import jax
import jax.numpy as jnp
from jax import lax
from jax.experimental import pallas as pl
from jax.experimental.pallas import tpu as pltpu
from jax.sharding import PartitionSpec as P

MESH = pl.DeviceIdType.MESH
LAG = 3
TILE = 1024


def ring_place(c, count):
    if count == 4:
        return c + (c // 2) * (1 - 2 * (c % 2))
    return c


def gather_kernel(rows, cols, halves, x_ref, counts_hbm, freq_hbm, val_band_hbm, cond_band_hbm, val_energy_hbm,
                  cond_energy_hbm, cols_ref, seg_ref, choose_ref, weights_ref, counts_ref, freq_ref, val_band, cond_band,
                  val_energy, cond_energy, small_sem, own_sem, line_send, line_recv, mate_send, mate_recv, enter_send,
                  relay_send, ring_recv):
    r, c = lax.axis_index("row"), lax.axis_index("col")
    chips = rows // 2
    q, k = r // 2, r % 2
    pieces, lane = cols_ref.shape[1], cols_ref.shape[3]
    ratio = rows // cols
    chunks = ratio * halves
    place = ring_place(c, cols)
    source = r // ratio
    ring_next = [ring_place((place + 1) % cols, cols), ring_place((place + cols - 1) % cols, cols)]
    ahead = (place - ring_place(source, cols) + cols) % cols
    hops = [ahead, cols - ahead]
    up_ok, down_ok = q + 1 < chips, q >= 1

    own = [
        pltpu.make_async_copy(x_ref.at[:, pl.ds(p * lane, lane)], cols_ref.at[r, p], own_sem.at[p])
        for p in range(pieces)
    ]
    small = [
        pltpu.make_async_copy(src, dst, small_sem.at[i])
        for i, (src, dst) in enumerate((
            (counts_hbm, counts_ref), (freq_hbm, freq_ref), (val_band_hbm, val_band), (cond_band_hbm, cond_band),
            (val_energy_hbm, val_energy), (cond_energy_hbm, cond_energy),
        ))
    ]
    for copy in own + small:
        copy.start()
    barrier = pltpu.get_barrier_semaphore()

    def greet(row, col):
        pl.semaphore_signal(barrier, inc=1, device_id=(row, col), device_id_type=MESH)

    mate = 2 * q + 1 - k
    greet(mate, c)
    for nxt in ring_next:
        greet(2 * q, nxt)
        greet(2 * q + 1, nxt)

    @pl.when(up_ok)
    def _():
        greet(r + 2, c)

    @pl.when(down_ok)
    def _():
        greet(r - 2, c)

    pl.semaphore_wait(barrier, 5 + up_ok.astype(jnp.int32) + down_ok.astype(jnp.int32))
    for copy in own:
        copy.wait()

    def remote(src, dst, send, recv, row, col):
        return pltpu.make_async_remote_copy(
            src_ref=src, dst_ref=dst, send_sem=send, recv_sem=recv, device_id=(row, col), device_id_type=MESH
        )

    def block_of(stream, d, core):
        return 2 * (q - d if stream == 0 else q + d) + core

    def has(stream, d):
        return q >= d if stream == 0 else q + d < chips

    def line_copy(stream, d, j, b):
        ref = cols_ref.at[b, pl.ds(2 * j, 2)]
        row = r + 2 if stream == 0 else r - 2
        return remote(ref, ref, line_send.at[stream, d, j], line_recv.at[stream, d, j], row, c)

    def line_arrival(stream, d, j, b):
        ref = cols_ref.at[b, pl.ds(2 * j, 2)]
        return remote(ref, ref, line_send.at[stream, d, j], line_recv.at[stream, d - 1, j], mate, c)

    def mate_copy(b, j):
        ref = cols_ref.at[b, pl.ds(2 * j, 2)]
        return remote(ref, ref, mate_send.at[b, j], mate_recv.at[b, j], mate, c)

    def enter_copy(b, j, way):
        g = c * ratio + j // halves
        src = cols_ref.at[b, 2 * j + way]
        dst = seg_ref.at[b, 2 * (j % halves) + way]
        return remote(src, dst, enter_send.at[b, j, way], ring_recv.at[b, j % halves, way], g, ring_next[way])

    def relay_copy(b, j, way):
        ref = seg_ref.at[b, 2 * (j % halves) + way]
        return remote(ref, ref, relay_send.at[b, j % halves, way], ring_recv.at[b, j % halves, way], r, ring_next[way])

    def feeds(j):
        return (c * ratio + j // halves) // 2 == q

    def relays(j):
        return (source != c) & (j // halves == r % ratio)

    def onward(stream):
        return up_ok if stream == 0 else down_ok

    def line_part(step):
        d, j = step // chunks, step % chunks
        for stream in (0, 1):
            here = has(stream, d) if stream == 0 else has(stream, d) & (d > 0)
            b = block_of(stream, d, k)

            @pl.when(has(stream, d))
            def _():
                @pl.when(d > 0)
                def _():
                    line_arrival(stream, d, j, b).wait_recv()

                @pl.when(onward(stream))
                def _():
                    line_copy(stream, d, j, b).start()

            @pl.when(here)
            def _():
                mate_copy(b, j).start()

                @pl.when(feeds(j))
                def _():
                    for way in (0, 1):
                        enter_copy(b, j, way).start()

    def ring_part(step, way):
        d, j = step // chunks, step % chunks

        @pl.when(relays(j))
        def _():
            for stream in (0, 1):
                here = has(stream, d) if stream == 0 else has(stream, d) & (d > 0)

                @pl.when(here)
                def _():
                    for core in (0, 1):
                        b = block_of(stream, d, core)
                        relay_copy(b, j, way).wait_recv()

                        @pl.when(ring_next[way] != source)
                        def _():
                            relay_copy(b, j, way).start()

    steps = chunks * chips

    def body(step, carry):
        @pl.when(step < steps)
        def _():
            line_part(step)

        for way in (0, 1):
            late = step - LAG * hops[way]

            @pl.when((late >= 0) & (late < steps))
            def _():
                ring_part(late, way)

        return carry

    lax.fori_loop(0, chunks, body, 0)
    for copy in small:
        copy.wait()
    capacity, (depth, slots) = x_ref.shape[0], choose_ref.shape
    place_of = slot_target(counts_ref, (1, slots), 1, capacity)
    choose = (lax.broadcasted_iota(jnp.int32, (depth, slots), 0) == place_of).astype(jnp.float32)
    gap = pick(cond_band, cond_energy) - pick(val_band, val_energy)
    gap = lax.dot_general(
        gap, choose, (((1,), (1,)), ((), ())), precision=lax.Precision.HIGHEST, preferred_element_type=jnp.float32
    )
    for f in range(weights_ref.shape[0]):
        weights_ref[f] = -4.0 * gap / (gap * gap + freq_ref[f] * freq_ref[f])
    choose_ref[...] = choose.astype(jnp.bfloat16)
    lax.fori_loop(chunks, steps + LAG * (cols - 1), body, 0)

    def finish(step, carry):
        d, j = step // chunks, step % chunks
        for stream in (0, 1):
            here = has(stream, d) if stream == 0 else has(stream, d) & (d > 0)
            b = block_of(stream, d, k)
            theirs = block_of(stream, d, 1 - k)

            @pl.when(has(stream, d) & onward(stream))
            def _():
                line_copy(stream, d, j, b).wait_send()

            @pl.when(here)
            def _():
                mate_copy(b, j).wait_send()
                mate_copy(theirs, j).wait_recv()

                @pl.when(feeds(j))
                def _():
                    for way in (0, 1):
                        enter_copy(b, j, way).wait_send()

                @pl.when(relays(j))
                def _():
                    for core in (0, 1):
                        e = block_of(stream, d, core)
                        for way in (0, 1):
                            @pl.when(ring_next[way] != source)
                            def _():
                                relay_copy(e, j, way).wait_send()

        return carry

    lax.fori_loop(0, steps, finish, 0)

    @pl.when(source == c)
    def _():
        here = pltpu.make_async_copy(cols_ref.at[:, pl.ds((r % ratio) * 2 * halves, 2 * halves)], seg_ref, own_sem.at[0])
        here.start()
        here.wait()


def gather(x, counts, frequency, val_band, cond_band, val_energy, cond_energy, rows, cols):
    capacity, width = x.shape
    slots = rows * capacity
    live = slots * 5 // 8
    depth = pl.cdiv(live, 256) * 256
    ratio = rows // cols
    seg_width = width // ratio
    halves = 2 if seg_width % 512 == 0 else 1
    chunks, chips = ratio * halves, rows // 2
    dma = pltpu.SemaphoreType.DMA
    return pl.pallas_call(
        functools.partial(gather_kernel, rows, cols, halves),
        out_shape=(
            pltpu.VMEM((rows, 2 * chunks, capacity, seg_width // halves // 2), x.dtype),
            pltpu.VMEM((rows, 2 * halves, capacity, seg_width // halves // 2), x.dtype),
            pltpu.VMEM((depth, slots), jnp.bfloat16),
            pltpu.VMEM((frequency.shape[0], 8, depth), jnp.float32),
        ),
        in_specs=[pl.BlockSpec(memory_space=pl.ANY)] * 7,
        out_specs=[pl.BlockSpec(memory_space=pltpu.VMEM)] * 4,
        scratch_shapes=[
            pltpu.SMEM(counts.shape, counts.dtype),
            pltpu.SMEM(frequency.shape, frequency.dtype),
            pltpu.VMEM(val_band.shape, val_band.dtype),
            pltpu.VMEM(cond_band.shape, cond_band.dtype),
            pltpu.VMEM(val_energy.shape, val_energy.dtype),
            pltpu.VMEM(cond_energy.shape, cond_energy.dtype),
            dma((6,)),
            dma((2 * chunks,)),
            dma((2, chips, chunks)),
            dma((2, chips, chunks)),
            dma((rows, chunks)),
            dma((rows, chunks)),
            dma((rows, chunks, 2)),
            dma((rows, halves, 2)),
            dma((rows, halves, 2)),
        ],
        compiler_params=pltpu.CompilerParams(
            collective_id=0, has_side_effects=True, vmem_limit_bytes=40 * 1024 * 1024
        ),
    )(x, counts, frequency, val_band, cond_band, val_energy, cond_energy)


def exact_dot(a, b):
    return lax.dot_general(
        a, b, (((1,), (0,)), ((), ())), precision=lax.Precision.HIGHEST, preferred_element_type=jnp.float32
    )


def pick(band_ref, table_ref):
    levels, slots = table_ref.shape[0], band_ref.shape[0]
    hit = lax.broadcasted_iota(jnp.int32, (levels, slots), 0) == band_ref[...][None, :]
    return exact_dot(jnp.broadcast_to(table_ref[...][None, :], (8, levels)), hit.astype(jnp.float32))


def slot_target(counts_ref, shape, axis, capacity):
    slot = lax.broadcasted_iota(jnp.int32, shape, axis)
    target = jnp.full(shape, -1, jnp.int32)
    before = 0
    for block in range(counts_ref.shape[0]):
        inside = slot - block * capacity
        live = (inside >= 0) & (inside < counts_ref[block])
        target = jnp.where(live, inside + before, target)
        before = before + counts_ref[block]
    return target


def product_kernel(weights, choose_ref, seg_ref, cols_ref, out_ref, packed, turned, scaled):
    which, n = pl.program_id(0), pl.program_id(1)
    tile = out_ref.shape[2]
    rows, pieces, capacity, lane = cols_ref.shape
    slots = rows * capacity

    @pl.when((n == 0) & (which == 0))
    def _():
        choose = choose_ref[...]
        for p in range(pieces):
            piece = cols_ref[:, p].reshape(slots, lane)
            packed[:, p * lane : (p + 1) * lane] = jnp.dot(
                choose, piece, preferred_element_type=jnp.float32
            ).astype(jnp.bfloat16)
        for p in range(seg_ref.shape[1]):
            piece = seg_ref[:, p].reshape(slots, lane)
            turned[p * lane : (p + 1) * lane, :] = lax.dot_general(
                piece, choose, (((0,), (1,)), ((), ())), preferred_element_type=jnp.float32
            ).astype(jnp.bfloat16)

    @pl.when(n == 0)
    def _():
        scaled[...] = (turned[...].astype(jnp.float32) * weights[which][:1]).astype(jnp.bfloat16)

    start = pl.multiple_of(n * tile, tile)
    out_ref[0] = jnp.dot(scaled[...], packed[:, pl.ds(start, tile)], preferred_element_type=jnp.float32)


def product(weights, choose, seg, columns):
    freqs = weights.shape[0]
    rows, pieces, capacity, lane = columns.shape
    width, seg_width = pieces * lane, seg.shape[1] * lane
    depth = choose.shape[0]
    tile = math.gcd(width, TILE)
    vmem = pl.BlockSpec(memory_space=pltpu.VMEM)
    return pl.pallas_call(
        product_kernel,
        out_shape=jax.ShapeDtypeStruct((freqs, seg_width, width), jnp.float32),
        grid=(freqs, width // tile),
        in_specs=[vmem] * 4,
        out_specs=pl.BlockSpec((1, seg_width, tile), lambda f, n: (f, 0, n)),
        scratch_shapes=[
            pltpu.VMEM((depth, width), jnp.bfloat16),
            pltpu.VMEM((seg_width, depth), jnp.bfloat16),
            pltpu.VMEM((seg_width, depth), jnp.bfloat16),
        ],
        compiler_params=pltpu.CompilerParams(vmem_limit_bytes=40 * 1024 * 1024),
    )(weights, choose, seg, columns)


def per_device(pair_elems, counts, val_band, cond_band, val_energy, cond_energy, frequency):
    rows, cols = lax.axis_size("row"), lax.axis_size("col")
    columns, seg, choose, weights = gather(
        pair_elems, counts, frequency, val_band, cond_band, val_energy, cond_energy, rows, cols
    )
    return product(weights, choose, seg, columns)


def solution(mesh):
    in_specs = (P("row", "col"), P(), P(), P(), P(), P(), P())
    out_specs = P(None, "row", "col")
    return jax.shard_map(
        per_device, mesh=mesh, in_specs=in_specs, out_specs=out_specs, check_vma=False
    )
```

profile of v0, /device:TPU:3, one launch (start us, length us, event | category | flops | bytes accessed | tf_op | source)
XLA Modules:
  0.0 57.5 jit_solution(3632057019535420808)
XLA Ops:
  0.0 0.0 copy-start
  0.0 0.9 %copy-done = bf16[40,3072]{1,0:T(8,128)(2,1)S(1)} copy-done((bf16[40,3072]{1,0:T(8,128)(2,1)S(1)}, bf16[40,3072]{1,0:T(8,128)(2,1)}, u32[]{:S(2)}) %copy-start) | copy-done | bytes 245784
  0.9 0.0 copy-start.1
  0.9 0.7 %copy-done.1 = s32[320]{0:T(512)S(1)} copy-done((s32[320]{0:T(512)S(1)}, s32[320]{0:T(512)}, u32[]{:S(2)}) %copy-start.1) | copy-done | bytes 1304
  1.6 0.0 copy-start.2
  1.6 0.7 %copy-done.2 = s32[320]{0:T(512)S(1)} copy-done((s32[320]{0:T(512)S(1)}, s32[320]{0:T(512)}, u32[]{:S(2)}) %copy-start.2) | copy-done | bytes 1304
  2.3 0.0 copy-start.3
  2.3 0.7 %copy-done.3 = f32[512]{0:T(512)S(1)} copy-done((f32[512]{0:T(512)S(1)}, f32[512]{0:T(512)}, u32[]{:S(2)}) %copy-start.3) | copy-done | bytes 2072
  3.0 0.0 copy-start.4
  3.0 0.7 %copy-done.4 = s32[8]{0:T(128)S(1)} copy-done((s32[8]{0:T(128)S(1)}, s32[8]{0:T(128)}, u32[]{:S(2)}) %copy-start.4) | copy-done | bytes 56
  3.6 0.0 copy-start.5
  3.6 0.7 %copy-done.5 = f32[3]{0:T(128)S(1)} copy-done((f32[3]{0:T(128)S(1)}, f32[3]{0:T(128)}, u32[]{:S(2)}) %copy-start.5) | copy-done | bytes 36
  4.3 0.0 copy-start.6
  4.3 0.7 %copy-done.6 = f32[128]{0:T(128)S(1)} copy-done((f32[128]{0:T(128)S(1)}, f32[128]{0:T(128)}, u32[]{:S(2)}) %copy-start.6) | copy-done | bytes 536
  5.0 31.8 %shard_map.73 = (bf16[8,8,40,384]{3,2,1,0:T(8,128)(2,1)S(1)}, bf16[8,4,40,384]{3,2,1,0:T(8,128)(2,1)S(1)}, bf16[256,320]{1,0:T(8,128)(2,1)S(1)}, f32[3,8,256]{2,1,0:T(8,128)S(1)}) custom-call(bf16[40,3072]{1,0:T(8,128)(2,1)S(1)} %copy-done, s32[8]{0:T(128)S(1)} %copy-done.4, f32[3]{0:T(128)S(1)} %copy-done.5, s32[320]{0:T(512)S(1)} %copy-done.1, ...), custom_call_target="tpu_custom_call" | custom-call | tf_op jit(solution)/shard_map/pallas_call | solution.py:243
  36.7 20.8 %shard_map.74 = f32[3,1536,3072]{2,1,0:T(8,128)} custom-call(f32[3,8,256]{2,1,0:T(8,128)S(1)} %get-tuple-element.9.weights, bf16[256,320]{1,0:T(8,128)(2,1)S(1)} %get-tuple-element.10.choose_ref, bf16[8,4,40,384]{3,2,1,0:T(8,128)(2,1)S(1)} %get-tuple-element.11.seg_ref, bf16[8,8,40,384]{3,2,1,0:T(8,128)(2,1)S(1)} %get-tuple-element.12.cols_ref), custom_call_target="tpu_custom_call" | custom-call | tf_op jit(solution)/shard_map/pallas_call | solution.py:335
Async XLA Ops:
  0.0 0.9 %copy-start = (bf16[40,3072]{1,0:T(8,128)(2,1)S(1)}, bf16[40,3072]{1,0:T(8,128)(2,1)}, u32[]{:S(2)}) copy-start(bf16[40,3072]{1,0:T(8,128)(2,1)} %x_ref.1) | copy-start | bytes 737284
  0.9 0.7 %copy-start.1 = (s32[320]{0:T(512)S(1)}, s32[320]{0:T(512)}, u32[]{:S(2)}) copy-start(s32[320]{0:T(512)} %val_band_hbm.1) | copy-start | bytes 3844
  1.6 0.7 %copy-start.2 = (s32[320]{0:T(512)S(1)}, s32[320]{0:T(512)}, u32[]{:S(2)}) copy-start(s32[320]{0:T(512)} %cond_band_hbm.1) | copy-start | bytes 3844
  2.3 0.7 %copy-start.3 = (f32[512]{0:T(512)S(1)}, f32[512]{0:T(512)}, u32[]{:S(2)}) copy-start(f32[512]{0:T(512)} %cond_energy_hbm.1) | copy-start | bytes 6148
  3.0 0.7 %copy-start.4 = (s32[8]{0:T(128)S(1)}, s32[8]{0:T(128)}, u32[]{:S(2)}) copy-start(s32[8]{0:T(128)} %counts_hbm.1) | copy-start | bytes 100
  3.6 0.7 %copy-start.5 = (f32[3]{0:T(128)S(1)}, f32[3]{0:T(128)}, u32[]{:S(2)}) copy-start(f32[3]{0:T(128)} %freq_hbm.1) | copy-start | bytes 40
  4.3 0.7 %copy-start.6 = (f32[128]{0:T(128)S(1)}, f32[128]{0:T(128)}, u32[]{:S(2)}) copy-start(f32[128]{0:T(128)} %val_energy_hbm.1) | copy-start | bytes 1540
where the time goes:
time: 57.8 us; the launch traced here: 57.5 us
  Pallas kernels  52.6 us (91%)
  local copies, waits for them, and re-layouts  4.95 us (9%)
    pallas_call x1, Pallas kernels, gather(): pl.pallas_call(functools.partial(gather_kernel, rows, cols, halves), out_...  31.8 us
    pallas_call x1, Pallas kernels, product(): pl.pallas_call(product_kernel, out_shape=jax.ShapeDtypeStruct((freqs, seg...  20.8 us
    unnamed x14, local copies, waits for them, and re-layouts  4.95 us

commit v1 on v0

--- a/solution.py
+++ b/solution.py
@@ -11,6 +11,8 @@
 MESH = pl.DeviceIdType.MESH
 LAG = 3
 TILE = 1024
+VMEM = 67043328
+SPARE = 1024 * 1024
 
 
 def ring_place(c, count):
@@ -240,6 +242,7 @@
     halves = 2 if seg_width % 512 == 0 else 1
     chunks, chips = ratio * halves, rows // 2
     dma = pltpu.SemaphoreType.DMA
+    room = 2 * (slots * (width + seg_width) + depth * slots) + 4 * 8 * depth * frequency.shape[0]
     return pl.pallas_call(
         functools.partial(gather_kernel, rows, cols, halves),
         out_shape=(
@@ -268,7 +271,7 @@
             dma((rows, halves, 2)),
         ],
         compiler_params=pltpu.CompilerParams(
-            collective_id=0, has_side_effects=True, vmem_limit_bytes=40 * 1024 * 1024
+            collective_id=0, has_side_effects=True, vmem_limit_bytes=VMEM - room - SPARE
         ),
     )(x, counts, frequency, val_band, cond_band, val_energy, cond_energy)
 

time: 57.8 us -> 52.7 us (0.912)
  local copies, waits for them, and re-layouts: 4.95 us -> 0 us
    unnamed x14 -> x0, local copies, waits for them, and re-layouts: 4.95 us -> none
where the time goes in v1:
time: 52.7 us; the launch traced here: 52.5 us
  Pallas kernels  52.5 us (100%)
    pallas_call x1, Pallas kernels, gather(): pl.pallas_call(functools.partial(gather_kernel, rows, cols, halves), out_...  31.7 us
    pallas_call x1, Pallas kernels, product(): pl.pallas_call(product_kernel, out_shape=jax.ShapeDtypeStruct((freqs, seg...  20.8 us

profile of v1, /device:TPU:3, one launch (start us, length us, event | category | flops | bytes accessed | tf_op | source)
XLA Modules:
  0.0 52.5 jit_solution(7551098435181251096)
XLA Ops:
  0.0 31.7 %shard_map.73 = (bf16[8,8,40,384]{3,2,1,0:T(8,128)(2,1)S(1)}, bf16[8,4,40,384]{3,2,1,0:T(8,128)(2,1)S(1)}, bf16[256,320]{1,0:T(8,128)(2,1)S(1)}, f32[3,8,256]{2,1,0:T(8,128)S(1)}) custom-call(bf16[40,3072]{1,0:T(8,128)(2,1)} %x_ref.1, s32[8]{0:T(128)} %counts_hbm.1, f32[3]{0:T(128)} %freq_hbm.1, s32[320]{0:T(512)} %val_band_hbm.1, s32[320]{0:T(512)} %cond_band_hbm.1, ...), custom_call_target="tpu_custom_call" | custom-call | tf_op jit(solution)/shard_map/pallas_call | solution.py:246
  31.7 20.8 %shard_map.74 = f32[3,1536,3072]{2,1,0:T(8,128)} custom-call(f32[3,8,256]{2,1,0:T(8,128)S(1)} %get-tuple-element.9.weights, bf16[256,320]{1,0:T(8,128)(2,1)S(1)} %get-tuple-element.10.choose_ref, bf16[8,4,40,384]{3,2,1,0:T(8,128)(2,1)S(1)} %get-tuple-element.11.seg_ref, bf16[8,8,40,384]{3,2,1,0:T(8,128)(2,1)S(1)} %get-tuple-element.12.cols_ref), custom_call_target="tpu_custom_call" | custom-call | tf_op jit(solution)/shard_map/pallas_call | solution.py:338

commit v2 on v1

--- a/solution.py
+++ b/solution.py
@@ -13,6 +13,11 @@
 TILE = 1024
 VMEM = 67043328
 SPARE = 1024 * 1024
+PIECES = 8
+PARTS = 4
+BUFFERS = 3
+END_LAG = 3
+MIDDLE_LAG = 4
 
 
 def ring_place(c, count):
@@ -350,8 +355,372 @@
     )(weights, choose, seg, columns)
 
 
+def plane_gather_kernel(rows, cols, x_ref, counts_hbm, freq_hbm, val_band_hbm, cond_band_hbm, val_energy_hbm,
+                        cond_energy_hbm, packed_ref, seg_ref, choose_ref, weights_ref, cols_ref, counts_ref, freq_ref,
+                        val_band, cond_band, val_energy, cond_energy, small_sem, own_sem, line_send, line_recv, mate_send,
+                        mate_recv, enter_send, relay_send, seg_recv):
+    r, c = lax.axis_index("row"), lax.axis_index("col")
+    chips = rows // 2
+    q, k = r // 2, r % 2
+    pieces, lane = cols_ref.shape[1], cols_ref.shape[3]
+    half = pieces // 2
+    place = ring_place(c, cols)
+    rel = (place - ring_place(q, cols) + cols) % cols
+    near = [ring_place((place + 1) % cols, cols), ring_place((place + cols - 1) % cols, cols)]
+    is_source = rel == 0
+    up_ok, down_ok = q + 1 < chips, q >= 1
+    lag = jnp.where(up_ok & down_ok, MIDDLE_LAG, END_LAG)
+
+    own = [
+        pltpu.make_async_copy(x_ref.at[:, pl.ds(p * lane, lane)], cols_ref.at[r, p], own_sem.at[p])
+        for p in range(pieces)
+    ]
+    small = [
+        pltpu.make_async_copy(src, dst, small_sem.at[i])
+        for i, (src, dst) in enumerate((
+            (counts_hbm, counts_ref), (freq_hbm, freq_ref), (val_band_hbm, val_band), (cond_band_hbm, cond_band),
+            (val_energy_hbm, val_energy), (cond_energy_hbm, cond_energy),
+        ))
+    ]
+    for copy in own + small:
+        copy.start()
+    barrier = pltpu.get_barrier_semaphore()
+
+    def greet(row, col):
+        pl.semaphore_signal(barrier, inc=1, device_id=(row, col), device_id_type=MESH)
+
+    mate = 2 * q + 1 - k
+    greet(mate, c)
+    for nxt in near:
+        greet(2 * q, nxt)
+        greet(2 * q + 1, nxt)
+
+    @pl.when(up_ok)
+    def _():
+        greet(r + 2, c)
+
+    @pl.when(down_ok)
+    def _():
+        greet(r - 2, c)
+
+    pl.semaphore_wait(barrier, 5 + up_ok.astype(jnp.int32) + down_ok.astype(jnp.int32))
+    for copy in own:
+        copy.wait()
+
+    def remote(src, dst, send, recv, row, col):
+        return pltpu.make_async_remote_copy(
+            src_ref=src, dst_ref=dst, send_sem=send, recv_sem=recv, device_id=(row, col), device_id_type=MESH
+        )
+
+    def block_of(stream, d, core):
+        return 2 * (q - d if stream == 0 else q + d) + core
+
+    def has(stream, d):
+        return q >= d if stream == 0 else q + d < chips
+
+    def here(stream, d):
+        return has(stream, d) if stream == 0 else has(stream, d) & (d > 0)
+
+    def onward(stream):
+        return up_ok if stream == 0 else down_ok
+
+    def line_copy(stream, d, piece, arrival):
+        row = r + 2 if stream == 0 else r - 2
+        return remote(piece, piece, line_send.at[stream, d], arrival, row, c)
+
+    def mate_copy(b, piece):
+        return remote(piece, piece, mate_send.at[b], mate_recv.at[b], mate, c)
+
+    def enter_copy(b, p, way):
+        arrival = seg_recv.at[b, jnp.where(p % 2 == way, p % half, half)]
+        return remote(cols_ref.at[b, p], seg_ref.at[b, p % half], enter_send.at[b], arrival, 2 * q + p // half, near[way])
+
+    def relay_copy(d, b, p, way):
+        last = (rel == 2) | tree(d)
+        piece = seg_ref.at[b, p % half]
+        return remote(piece, piece, relay_send.at[b], seg_recv.at[b, jnp.where(last, half, p % half)], r, near[way])
+
+    def await_sends(ref, sem):
+        remote(ref, ref, sem, mate_recv.at[0], mate, c).wait_send()
+
+    def await_arrivals(ref, sem):
+        remote(ref, ref, mate_send.at[0], sem, mate, c).wait_recv()
+
+    def tree(d):
+        return d == chips - 1
+
+    def enters(d, p, way):
+        return (p % 2 == way) | tree(d)
+
+    def forwards(d, p, way):
+        return (p % 2 == way) & ((rel == (1 if way == 0 else cols - 1)) | ((rel == 2) & ~tree(d)))
+
+    def feed(d, p, b):
+        @pl.when(is_source)
+        def _():
+            for way in (0, 1):
+                @pl.when(enters(d, p, way))
+                def _():
+                    enter_copy(b, p, way).start()
+
+    def begin(p, carry):
+        for stream in (0, 1):
+            @pl.when(onward(stream))
+            def _():
+                line_copy(stream, 0, cols_ref.at[r, p], line_recv.at[stream, 0, p]).start()
+
+        feed(0, p, r)
+        mate_copy(r, cols_ref.at[r, p]).start()
+        return carry
+
+    lax.fori_loop(0, pieces, begin, 0)
+
+    for copy in small:
+        copy.wait()
+    capacity, (depth, slots) = x_ref.shape[0], choose_ref.shape
+    place_of = slot_target(counts_ref, (1, slots), 1, capacity)
+    choose = (lax.broadcasted_iota(jnp.int32, (depth, slots), 0) == place_of).astype(jnp.float32)
+    gap = pick(cond_band, cond_energy) - pick(val_band, val_energy)
+    gap = lax.dot_general(
+        gap, choose, (((1,), (1,)), ((), ())), precision=lax.Precision.HIGHEST, preferred_element_type=jnp.float32
+    )
+    for f in range(weights_ref.shape[0]):
+        weights_ref[f] = -4.0 * gap / (gap * gap + freq_ref[f] * freq_ref[f])
+    choose_ref[...] = choose.astype(jnp.bfloat16)
+
+    def line_part(step):
+        d, p = step // pieces + 1, step % pieces
+        for stream in (0, 1):
+            b = block_of(stream, d, k)
+
+            @pl.when(has(stream, d))
+            def _():
+                piece = cols_ref.at[b, p]
+                await_arrivals(piece, line_recv.at[stream, d - 1, p])
+
+                @pl.when(onward(stream))
+                def _():
+                    line_copy(stream, d, piece, line_recv.at[stream, d, p]).start()
+
+                feed(d, p, b)
+                mate_copy(b, piece).start()
+
+    def relay_part(step, way):
+        d, p = step // pieces, step % pieces
+
+        @pl.when((p // half == k) & forwards(d, p, way))
+        def _():
+            for stream in (0, 1):
+                @pl.when(here(stream, d))
+                def _():
+                    for core in (0, 1):
+                        b = block_of(stream, d, core)
+                        await_arrivals(seg_ref.at[b, p % half], seg_recv.at[b, p % half])
+                        relay_copy(d, b, p, way).start()
+
+    steps = pieces * (chips - 1)
+    delay = lag * jnp.where(rel == 2, 2, 1)
+
+    def body(step, carry):
+        @pl.when((step >= 0) & (step < steps))
+        def _():
+            line_part(step)
+
+        late = step - delay + pieces
+        for way in (0, 1):
+            @pl.when((late >= 0) & (late < steps + pieces))
+            def _():
+                relay_part(late, way)
+
+        return carry
+
+    lax.fori_loop(jnp.minimum(delay - pieces, 0), steps + delay, body, 0)
+
+    def gather_end(d, carry):
+        for stream in (0, 1):
+            @pl.when(here(stream, d))
+            def _():
+                b = block_of(stream, d, 1 - k)
+                await_arrivals(cols_ref.at[b], mate_recv.at[b])
+
+        return carry
+
+    lax.fori_loop(0, chips, gather_end, 0)
+    stay = pltpu.make_async_copy(cols_ref.at[:, pl.ds(k * half, half)], seg_ref, own_sem.at[0])
+
+    @pl.when(is_source)
+    def _():
+        stay.start()
+
+    choice = choose_ref[...]
+    for p in range(pieces):
+        piece = cols_ref[:, p].reshape(slots, lane)
+        packed_ref[:, p * lane : (p + 1) * lane] = jnp.dot(
+            choice, piece, preferred_element_type=jnp.float32
+        ).astype(jnp.bfloat16)
+
+    def finish(d, carry):
+        for stream in (0, 1):
+            b = block_of(stream, d, k)
+
+            @pl.when(has(stream, d) & onward(stream))
+            def _():
+                await_sends(cols_ref.at[b], line_send.at[stream, d])
+
+            @pl.when(here(stream, d))
+            def _():
+                await_sends(cols_ref.at[b], mate_send.at[b])
+
+                @pl.when(is_source & tree(d))
+                def _():
+                    await_sends(cols_ref.at[pl.ds(0, 2)], enter_send.at[b])
+
+                @pl.when(is_source & ~tree(d))
+                def _():
+                    await_sends(cols_ref.at[b], enter_send.at[b])
+
+                for core in (0, 1):
+                    e = block_of(stream, d, core)
+
+                    @pl.when((rel == 1) | (rel == cols - 1))
+                    def _():
+                        await_sends(seg_ref.at[e, pl.ds(0, half // 2)], relay_send.at[e])
+                        await_arrivals(seg_ref.at[e, pl.ds(0, half // 2)], seg_recv.at[e, half])
+
+                    @pl.when((rel == 2) & ~tree(d))
+                    def _():
+                        await_sends(seg_ref.at[e], relay_send.at[e])
+
+                    @pl.when((rel == 2) & tree(d))
+                    def _():
+                        await_arrivals(seg_ref.at[e], seg_recv.at[e, half])
+
+        return carry
+
+    lax.fori_loop(0, chips, finish, 0)
+
+    @pl.when(is_source)
+    def _():
+        stay.wait()
+
+
+def plane_gather(x, counts, frequency, val_band, cond_band, val_energy, cond_energy, rows, cols):
+    capacity, width = x.shape
+    slots = rows * capacity
+    depth = pl.cdiv(slots * 5 // 8, 256) * 256
+    chips, pieces = rows // 2, PIECES
+    half, lane, freqs = pieces // 2, width // pieces, frequency.shape[0]
+    dma = pltpu.SemaphoreType.DMA
+    room = 2 * (slots * width // 2 + depth * (width + slots)) + 4 * 8 * depth * freqs
+    return pl.pallas_call(
+        functools.partial(plane_gather_kernel, rows, cols),
+        out_shape=(
+            pltpu.VMEM((depth, width), x.dtype),
+            pltpu.VMEM((rows, half, capacity, lane), x.dtype),
+            pltpu.VMEM((depth, slots), jnp.bfloat16),
+            pltpu.VMEM((freqs, 8, depth), jnp.float32),
+        ),
+        in_specs=[pl.BlockSpec(memory_space=pl.ANY)] * 7,
+        out_specs=[pl.BlockSpec(memory_space=pltpu.VMEM)] * 4,
+        scratch_shapes=[
+            pltpu.VMEM((rows, pieces, capacity, lane), x.dtype),
+            pltpu.SMEM(counts.shape, counts.dtype),
+            pltpu.SMEM(frequency.shape, frequency.dtype),
+            pltpu.VMEM(val_band.shape, val_band.dtype),
+            pltpu.VMEM(cond_band.shape, cond_band.dtype),
+            pltpu.VMEM(val_energy.shape, val_energy.dtype),
+            pltpu.VMEM(cond_energy.shape, cond_energy.dtype),
+            dma((6,)),
+            dma((pieces,)),
+            dma((2, chips)),
+            dma((2, chips, pieces)),
+            dma((rows,)),
+            dma((rows,)),
+            dma((rows,)),
+            dma((rows,)),
+            dma((rows, half + 1)),
+        ],
+        compiler_params=pltpu.CompilerParams(
+            collective_id=0, has_side_effects=True, vmem_limit_bytes=VMEM - room - SPARE
+        ),
+    )(x, counts, frequency, val_band, cond_band, val_energy, cond_energy)
+
+
+def stream_kernel(weights, choose_ref, seg_ref, packed_ref, out_ref, turned, buf, sem):
+    freqs, depth = weights.shape[0], choose_ref.shape[0]
+    rows, chunks, capacity, lane = seg_ref.shape
+    depth_slots = rows * capacity
+    slots, part = buf.shape[0], buf.shape[2] // sem.shape[1]
+    total = chunks * freqs
+
+    def put(t, n):
+        tall = pl.ds(pl.multiple_of((t // freqs) * lane, lane), lane)
+        return pltpu.make_async_copy(
+            buf.at[t % slots, :, pl.ds(n * part, part)],
+            out_ref.at[t % freqs, tall, pl.ds(n * part, part)],
+            sem.at[t % slots, n],
+        )
+
+    def body(t, carry):
+        chunk, f = t // freqs, t % freqs
+
+        @pl.when(f == 0)
+        def _():
+            piece = seg_ref[:, chunk].reshape(depth_slots, lane)
+            turned[...] = lax.dot_general(
+                piece, choose_ref[...], (((0,), (1,)), ((), ())), preferred_element_type=jnp.float32
+            )
+
+        scaled = (turned[...] * weights[f][:1]).astype(jnp.bfloat16)
+        for n in range(sem.shape[1]):
+            @pl.when(t >= slots)
+            def _():
+                put(t - slots, n).wait()
+
+            buf[t % slots, :, n * part : (n + 1) * part] = jnp.dot(
+                scaled, packed_ref[:, n * part : (n + 1) * part], preferred_element_type=jnp.float32
+            )
+            put(t, n).start()
+
+        return carry
+
+    lax.fori_loop(0, total, body, 0)
+
+    def drain(t, carry):
+        for n in range(sem.shape[1]):
+            put(t, n).wait()
+        return carry
+
+    lax.fori_loop(max(total - slots, 0), total, drain, 0)
+
+
+def stream_product(weights, choose, seg, packed):
+    freqs = weights.shape[0]
+    rows, chunks, capacity, lane = seg.shape
+    depth, width = packed.shape
+    parts = PARTS
+    vmem = pl.BlockSpec(memory_space=pltpu.VMEM)
+    return pl.pallas_call(
+        stream_kernel,
+        out_shape=jax.ShapeDtypeStruct((freqs, chunks * lane, width), jnp.float32),
+        in_specs=[vmem] * 4,
+        out_specs=pl.BlockSpec(memory_space=pl.ANY),
+        scratch_shapes=[
+            pltpu.VMEM((lane, depth), jnp.float32),
+            pltpu.VMEM((BUFFERS, lane, width), jnp.float32),
+            pltpu.SemaphoreType.DMA((BUFFERS, parts)),
+        ],
+        compiler_params=pltpu.CompilerParams(vmem_limit_bytes=40 * 1024 * 1024),
+    )(weights, choose, seg, packed)
+
+
 def per_device(pair_elems, counts, val_band, cond_band, val_energy, cond_energy, frequency):
     rows, cols = lax.axis_size("row"), lax.axis_size("col")
+    if cols == 4 and rows == 2 * cols and pair_elems.shape[1] % (128 * PIECES) == 0:
+        packed, seg, choose, weights = plane_gather(
+            pair_elems, counts, frequency, val_band, cond_band, val_energy, cond_energy, rows, cols
+        )
+        return stream_product(weights, choose, seg, packed)
     columns, seg, choose, weights = gather(
         pair_elems, counts, frequency, val_band, cond_band, val_energy, cond_energy, rows, cols
     )

time: 52.7 us -> 47 us (0.89)
  the two profiles are of different devices: /device:TPU:3 before, /device:TPU:25 now
where the time goes in v2:
time: 47 us; the launch traced here: 46.9 us
  Pallas kernels  46.9 us (100%)
    pallas_call x1, Pallas kernels, plane_gather(): pl.pallas_call(functools.partial(plane_gather_kernel, rows, cols), out_sh...  26.7 us
    pallas_call x1, Pallas kernels, stream_product(): pl.pallas_call(stream_kernel, out_shape=jax.ShapeDtypeStruct((freqs, chun...  20.2 us

profile of v2, /device:TPU:25, one launch (start us, length us, event | category | flops | bytes accessed | tf_op | source)
XLA Modules:
  0.0 46.9 jit_solution(99459454606995934)
XLA Ops:
  0.0 26.7 %shard_map.73 = (bf16[256,3072]{1,0:T(8,128)(2,1)S(1)}, bf16[8,4,40,384]{3,2,1,0:T(8,128)(2,1)S(1)}, bf16[256,320]{1,0:T(8,128)(2,1)S(1)}, f32[3,8,256]{2,1,0:T(8,128)S(1)}) custom-call(bf16[40,3072]{1,0:T(8,128)(2,1)} %x_ref.1, s32[8]{0:T(128)} %counts_hbm.1, f32[3]{0:T(128)} %freq_hbm.1, s32[320]{0:T(512)} %val_band_hbm.1, s32[320]{0:T(512)} %cond_band_hbm.1, ...), custom_call_target="tpu_custom_call" | custom-call | tf_op jit(solution)/shard_map/pallas_call | solution.py:615
  26.7 20.2 %shard_map.74 = f32[3,1536,3072]{2,1,0:T(8,128)} custom-call(f32[3,8,256]{2,1,0:T(8,128)S(1)} %get-tuple-element.9.weights, bf16[256,320]{1,0:T(8,128)(2,1)S(1)} %get-tuple-element.10.choose_ref, bf16[8,4,40,384]{3,2,1,0:T(8,128)(2,1)S(1)} %get-tuple-element.11.seg_ref, bf16[256,3072]{1,0:T(8,128)(2,1)S(1)} %get-tuple-element.12.packed_ref), custom_call_target="tpu_custom_call" | custom-call | tf_op jit(solution)/shard_map/pallas_call | solution.py:703

commit v3 on v2

--- a/solution.py
+++ b/solution.py
@@ -14,10 +14,11 @@
 VMEM = 67043328
 SPARE = 1024 * 1024
 PIECES = 8
-PARTS = 4
-BUFFERS = 3
-END_LAG = 3
-MIDDLE_LAG = 4
+PARTS = 2
+FIRST_PARTS = 4
+ROLE_DELAYS = {True: {False: (3, -1), True: (6, 2)}, False: {False: (8, 8), True: (16, 16)}}
+HOLD_STEP = 3
+SPREAD_STEP = 11
 
 
 def ring_place(c, count):
@@ -356,9 +357,10 @@
 
 
 def plane_gather_kernel(rows, cols, x_ref, counts_hbm, freq_hbm, val_band_hbm, cond_band_hbm, val_energy_hbm,
-                        cond_energy_hbm, packed_ref, seg_ref, choose_ref, weights_ref, cols_ref, counts_ref, freq_ref,
+                        cond_energy_hbm, cols_ref, seg_ref, choose_ref, weights_ref, counts_ref, freq_ref,
                         val_band, cond_band, val_energy, cond_energy, small_sem, own_sem, line_send, line_recv, mate_send,
-                        mate_recv, enter_send, relay_send, seg_recv):
+                        mate_recv, enter_send, relay_send, seg_recv, held, held_send, held_recv, aid_send,
+                        aid_recv, aid_mate_send, aid_mate_recv):
     r, c = lax.axis_index("row"), lax.axis_index("col")
     chips = rows // 2
     q, k = r // 2, r % 2
@@ -366,10 +368,19 @@
     half = pieces // 2
     place = ring_place(c, cols)
     rel = (place - ring_place(q, cols) + cols) % cols
-    near = [ring_place((place + 1) % cols, cols), ring_place((place + cols - 1) % cols, cols)]
+
+    def chip_at(position):
+        return ring_place((position + cols) % cols, cols)
+
+    near = [chip_at(place + 1), chip_at(place - 1)]
     is_source = rel == 0
     up_ok, down_ok = q + 1 < chips, q >= 1
-    lag = jnp.where(up_ok & down_ok, MIDDLE_LAG, END_LAG)
+    end = ~(up_ok & down_ok)
+    target = jnp.where(q == 1, 0, chips - 1)
+    target_rel = (place - ring_place(target, cols) + cols) % cols
+    helper = ((q == 1) | (q == chips - 2)) & ~end
+    beside = jnp.where(q == 0, 1, chips - 2)
+    aids = [(h * half + half // 2, cols - 1) for h in (0, 1)] + [(h * half + half // 2 + 1, 2) for h in (0, 1)]
 
     own = [
         pltpu.make_async_copy(x_ref.at[:, pl.ds(p * lane, lane)], cols_ref.at[r, p], own_sem.at[p])
@@ -391,9 +402,17 @@
 
     mate = 2 * q + 1 - k
     greet(mate, c)
-    for nxt in near:
-        greet(2 * q, nxt)
-        greet(2 * q + 1, nxt)
+    for turn in range(1, cols):
+        greet(r, chip_at(place + turn))
+
+    @pl.when(is_source)
+    def _():
+        greet(mate, near[0])
+        greet(mate, near[1])
+
+    @pl.when(rel % 2 == 1)
+    def _():
+        greet(mate, chip_at(place - rel))
 
     @pl.when(up_ok)
     def _():
@@ -403,7 +422,14 @@
     def _():
         greet(r - 2, c)
 
-    pl.semaphore_wait(barrier, 5 + up_ok.astype(jnp.int32) + down_ok.astype(jnp.int32))
+    crossing = (end & ~is_source) | (helper & (target_rel != 0))
+
+    @pl.when(crossing)
+    def _():
+        greet(2 * jnp.where(end, beside, target) + 1 - k, c)
+
+    calls = cols + jnp.where(is_source, 2, rel % 2) + (up_ok.astype(jnp.int32) + down_ok.astype(jnp.int32))
+    pl.semaphore_wait(barrier, calls + crossing.astype(jnp.int32))
     for copy in own:
         copy.wait()
 
@@ -447,13 +473,37 @@
         remote(ref, ref, mate_send.at[0], sem, mate, c).wait_recv()
 
     def tree(d):
-        return d == chips - 1
+        return d == jnp.maximum(q, chips - 1 - q)
+
+    def aided(d, p):
+        return end & (d == 1) & (p % half >= half // 2)
 
     def enters(d, p, way):
         return (p % 2 == way) | tree(d)
 
     def forwards(d, p, way):
-        return (p % 2 == way) & ((rel == (1 if way == 0 else cols - 1)) | ((rel == 2) & ~tree(d)))
+        carries = (rel == (1 if way == 0 else cols - 1)) | ((rel == 2) & ~tree(d))
+        return (p % 2 == way) & carries & ~aided(d, p)
+
+    def held_copy(i, p, line):
+        dst = held.at[i]
+        return remote(cols_ref.at[r, p], dst, held_send, held_recv.at[i], r, chip_at(place + line))
+
+    def aid_line_copy(i, p):
+        b = r
+        dst = seg_ref.at[b, p % half]
+        return remote(held.at[i], dst, held_send, seg_recv.at[b, p % half], 2 * target + p // half, c)
+
+    def aid_copy(b, p, turn):
+        piece = seg_ref.at[b, p % half]
+        return remote(piece, piece, aid_send, seg_recv.at[b, p % half], r, chip_at(place + turn))
+
+    def aid_home_copy(i, core, b, p, line):
+        return remote(seg_ref.at[b, p % half], cols_ref.at[b, p], aid_send, aid_recv.at[i, core], r, chip_at(place - line))
+
+    def aid_mate_copy(b, p):
+        piece = cols_ref.at[b, p]
+        return remote(piece, piece, aid_mate_send, aid_mate_recv, mate, c)
 
     def feed(d, p, b):
         @pl.when(is_source)
@@ -465,13 +515,21 @@
 
     def begin(p, carry):
         for stream in (0, 1):
-            @pl.when(onward(stream))
+            toward = target > q if stream == 0 else target < q
+            spared = helper & (target_rel == 0) & toward & (p % half >= half // 2)
+
+            @pl.when(onward(stream) & ~spared)
             def _():
                 line_copy(stream, 0, cols_ref.at[r, p], line_recv.at[stream, 0, p]).start()
 
         feed(0, p, r)
         mate_copy(r, cols_ref.at[r, p]).start()
         return carry
+
+    @pl.when(helper & (target_rel == 0))
+    def _():
+        for i, (p, line) in enumerate(aids):
+            held_copy(i, p, line).start()
 
     lax.fori_loop(0, pieces, begin, 0)
 
@@ -488,114 +546,236 @@
         weights_ref[f] = -4.0 * gap / (gap * gap + freq_ref[f] * freq_ref[f])
     choose_ref[...] = choose.astype(jnp.bfloat16)
 
-    def line_part(step):
-        d, p = step // pieces + 1, step % pieces
-        for stream in (0, 1):
-            b = block_of(stream, d, k)
-
-            @pl.when(has(stream, d))
+    def hold_part():
+        for i, (p, line) in enumerate(aids):
+            @pl.when(helper & (target_rel == line))
+            def _():
+                await_arrivals(held.at[i], held_recv.at[i])
+                aid_line_copy(i, p).start()
+
+    def spread_part():
+        for i, (p, line) in enumerate(aids):
+            @pl.when(end & (rel == line) & (k == p // half))
+            def _():
+                for core in (0, 1):
+                    b = 2 * beside + core
+                    await_arrivals(seg_ref.at[b, p % half], seg_recv.at[b, p % half])
+                    aid_home_copy(i, core, b, p, line).start()
+                    for turn in range(1, cols):
+                        if (line + turn) % cols != 0:
+                            aid_copy(b, p, turn).start()
+
+    def land_part():
+        for i, (p, line) in enumerate(aids):
+            @pl.when(end & is_source & (k == p // half))
+            def _():
+                for core in (0, 1):
+                    b = 2 * beside + core
+                    await_arrivals(cols_ref.at[b, p], aid_recv.at[i, core])
+                    aid_mate_copy(b, p).start()
+
+    def line_step(d, p, ends, source):
+        if ends:
+            flow = jnp.where(q == 0, 1, 0)
+            streams = [(flow, 2 * (q + jnp.where(q == 0, d, -d)) + k, None, (d > 0) & (d < chips))]
+        else:
+            streams = [
+                (0, 2 * (q - d) + k, r + 2, (d > 0) & (d <= q)),
+                (1, 2 * (q + d) + k, r - 2, (d > 0) & (d < chips - q)),
+            ]
+        for stream, b, row, present in streams:
+            if ends and source and p % half >= half // 2:
+                present = present & (d > 1)
+
+            @pl.when(present)
             def _():
                 piece = cols_ref.at[b, p]
                 await_arrivals(piece, line_recv.at[stream, d - 1, p])
-
-                @pl.when(onward(stream))
-                def _():
-                    line_copy(stream, d, piece, line_recv.at[stream, d, p]).start()
-
-                feed(d, p, b)
+                if row is not None:
+                    remote(piece, piece, line_send.at[stream, d], line_recv.at[stream, d, p], row, c).start()
+                if source:
+                    enter_copy(b, p, p % 2).start()
+
+                    @pl.when(tree(d))
+                    def _():
+                        enter_copy(b, p, 1 - p % 2).start()
+
                 mate_copy(b, piece).start()
 
-    def relay_part(step, way):
-        d, p = step // pieces, step % pieces
-
-        @pl.when((p // half == k) & forwards(d, p, way))
+    def relay_step(d, p, ends, opposite, least, most):
+        mine = k == p // half
+        if ends:
+            blocks = [(2 * (q + jnp.where(q == 0, d, -d)), (d >= least) & (d <= most))]
+            if p % half >= half // 2:
+                mine = mine & (d != 1)
+        else:
+            blocks = [(2 * (q - d), (d >= least) & (d <= most) & (d <= q)), (2 * (q + d), (d >= least) & (d <= most) & (d > 0) & (d < chips - q))]
+        if opposite:
+            mine = mine & ~tree(d)
+        else:
+            mine = mine & (rel == (1 if p % 2 == 0 else cols - 1))
+
+        @pl.when(mine)
         def _():
-            for stream in (0, 1):
-                @pl.when(here(stream, d))
+            for first, present in blocks:
+                @pl.when(present)
                 def _():
                     for core in (0, 1):
-                        b = block_of(stream, d, core)
+                        b = first + core
                         await_arrivals(seg_ref.at[b, p % half], seg_recv.at[b, p % half])
-                        relay_copy(d, b, p, way).start()
-
-    steps = pieces * (chips - 1)
-    delay = lag * jnp.where(rel == 2, 2, 1)
-
-    def body(step, carry):
-        @pl.when((step >= 0) & (step < steps))
-        def _():
-            line_part(step)
-
-        late = step - delay + pieces
-        for way in (0, 1):
-            @pl.when((late >= 0) & (late < steps + pieces))
-            def _():
-                relay_part(late, way)
-
-        return carry
-
-    lax.fori_loop(jnp.minimum(delay - pieces, 0), steps + delay, body, 0)
+                        relay_copy(d, b, p, p % 2).start()
+
+    def role(ends, place_in_ring):
+        source, opposite = place_in_ring == 0, place_in_ring == 2
+        near_delay, far_delay = ROLE_DELAYS[ends][opposite]
+
+        def body(d, carry):
+            for p in range(pieces):
+                line_step(d, p, ends, source)
+                step = d - 1
+                if not ends and p == HOLD_STEP % pieces:
+                    @pl.when(step == HOLD_STEP // pieces)
+                    def _():
+                        hold_part()
+
+                if ends and not source and p == SPREAD_STEP % pieces:
+                    @pl.when(step == SPREAD_STEP // pieces)
+                    def _():
+                        spread_part()
+
+                if not source:
+                    for delay, least, most in ((near_delay, 0, 1), (far_delay, 2, chips - 1)):
+                        shift, late = divmod(p - delay, pieces)
+                        relay_step(d + shift, late, ends, opposite, least, most)
+
+            return carry
+
+        turns = 0 if source else max(0, -(-max(near_delay, far_delay) // pieces))
+        start = 1 if source else 0
+        lax.fori_loop(start, chips + turns, body, 0)
+
+    for ends in (False, True):
+        for kind in (0, 1, 2):
+            here_now = (rel == kind) if kind != 1 else (rel % 2 == 1)
+
+            @pl.when(here_now & (end if ends else ~end))
+            def _():
+                role(ends, kind)
+
+    @pl.when(end & is_source)
+    def _():
+        land_part()
 
     def gather_end(d, carry):
         for stream in (0, 1):
             @pl.when(here(stream, d))
             def _():
                 b = block_of(stream, d, 1 - k)
-                await_arrivals(cols_ref.at[b], mate_recv.at[b])
+                partial = is_source & aided(d, pieces - 1)
+
+                @pl.when(partial)
+                def _():
+                    await_arrivals(cols_ref.at[b, pl.ds(0, half)], mate_recv.at[b])
+
+                @pl.when(~partial)
+                def _():
+                    await_arrivals(cols_ref.at[b], mate_recv.at[b])
 
         return carry
 
     lax.fori_loop(0, chips, gather_end, 0)
+
+    @pl.when(end & is_source)
+    def _():
+        await_arrivals(cols_ref.at[0, pl.ds(0, half)], aid_mate_recv)
+
     stay = pltpu.make_async_copy(cols_ref.at[:, pl.ds(k * half, half)], seg_ref, own_sem.at[0])
 
     @pl.when(is_source)
     def _():
         stay.start()
 
-    choice = choose_ref[...]
-    for p in range(pieces):
-        piece = cols_ref[:, p].reshape(slots, lane)
-        packed_ref[:, p * lane : (p + 1) * lane] = jnp.dot(
-            choice, piece, preferred_element_type=jnp.float32
-        ).astype(jnp.bfloat16)
-
     def finish(d, carry):
+        part = aided(d, pieces - 1)
         for stream in (0, 1):
             b = block_of(stream, d, k)
-
-            @pl.when(has(stream, d) & onward(stream))
+            toward = target > q if stream == 0 else target < q
+            spared = helper & (target_rel == 0) & toward & (d == 0)
+
+            @pl.when(has(stream, d) & onward(stream) & spared)
+            def _():
+                await_sends(cols_ref.at[b, pl.ds(0, half)], line_send.at[stream, d])
+
+            @pl.when(has(stream, d) & onward(stream) & ~spared)
             def _():
                 await_sends(cols_ref.at[b], line_send.at[stream, d])
 
             @pl.when(here(stream, d))
             def _():
-                await_sends(cols_ref.at[b], mate_send.at[b])
+                @pl.when(is_source & part)
+                def _():
+                    await_sends(cols_ref.at[b, pl.ds(0, half)], mate_send.at[b])
+                    await_sends(cols_ref.at[b, pl.ds(0, half)], enter_send.at[b])
+
+                @pl.when(~(is_source & part))
+                def _():
+                    await_sends(cols_ref.at[b], mate_send.at[b])
 
                 @pl.when(is_source & tree(d))
                 def _():
                     await_sends(cols_ref.at[pl.ds(0, 2)], enter_send.at[b])
 
-                @pl.when(is_source & ~tree(d))
+                @pl.when(is_source & ~tree(d) & ~part)
                 def _():
                     await_sends(cols_ref.at[b], enter_send.at[b])
 
                 for core in (0, 1):
                     e = block_of(stream, d, core)
-
-                    @pl.when((rel == 1) | (rel == cols - 1))
-                    def _():
-                        await_sends(seg_ref.at[e, pl.ds(0, half // 2)], relay_send.at[e])
-                        await_arrivals(seg_ref.at[e, pl.ds(0, half // 2)], seg_recv.at[e, half])
-
-                    @pl.when((rel == 2) & ~tree(d))
-                    def _():
-                        await_sends(seg_ref.at[e], relay_send.at[e])
+                    for some, count in ((part, half // 2), (~part, half)):
+                        @pl.when(some & ((rel == 1) | (rel == cols - 1)))
+                        def _():
+                            await_sends(seg_ref.at[e, pl.ds(0, count // 2)], relay_send.at[e])
+                            await_arrivals(seg_ref.at[e, pl.ds(0, count // 2)], seg_recv.at[e, half])
+
+                        @pl.when(some & (rel == 2) & ~tree(d))
+                        def _():
+                            await_sends(seg_ref.at[e, pl.ds(0, count)], relay_send.at[e])
 
                     @pl.when((rel == 2) & tree(d))
                     def _():
                         await_arrivals(seg_ref.at[e], seg_recv.at[e, half])
 
         return carry
+
+    for i, (p, line) in enumerate(aids):
+        @pl.when(end & ~is_source & (rel != line) & (k == p // half))
+        def _():
+            for core in (0, 1):
+                b = 2 * beside + core
+                await_arrivals(seg_ref.at[b, p % half], seg_recv.at[b, p % half])
+
+    for line in range(1, cols):
+        for core in (0, 1):
+            count = sum(1 for p, other in aids if other == line and p // half == core)
+            if count > 0:
+                @pl.when(end & (rel == line) & (k == core))
+                def _():
+                    await_sends(cols_ref.at[pl.ds(0, cols - 1), pl.ds(0, 2 * count)], aid_send)
+
+    for line in range(1, cols):
+        count = sum(1 for _, other in aids if other == line)
+        if count > 0:
+            @pl.when(helper & (target_rel == line))
+            def _():
+                await_sends(held.at[pl.ds(0, count)], held_send)
+
+    @pl.when(helper & (target_rel == 0))
+    def _():
+        await_sends(held, held_send)
+
+    @pl.when(end & is_source)
+    def _():
+        await_sends(cols_ref.at[0, pl.ds(0, half)], aid_mate_send)
 
     lax.fori_loop(0, chips, finish, 0)
 
@@ -611,11 +791,11 @@
     chips, pieces = rows // 2, PIECES
     half, lane, freqs = pieces // 2, width // pieces, frequency.shape[0]
     dma = pltpu.SemaphoreType.DMA
-    room = 2 * (slots * width // 2 + depth * (width + slots)) + 4 * 8 * depth * freqs
+    room = 2 * (slots * width * 3 // 2 + depth * slots) + 4 * 8 * depth * freqs
     return pl.pallas_call(
         functools.partial(plane_gather_kernel, rows, cols),
         out_shape=(
-            pltpu.VMEM((depth, width), x.dtype),
+            pltpu.VMEM((rows, pieces, capacity, lane), x.dtype),
             pltpu.VMEM((rows, half, capacity, lane), x.dtype),
             pltpu.VMEM((depth, slots), jnp.bfloat16),
             pltpu.VMEM((freqs, 8, depth), jnp.float32),
@@ -623,7 +803,6 @@
         in_specs=[pl.BlockSpec(memory_space=pl.ANY)] * 7,
         out_specs=[pl.BlockSpec(memory_space=pltpu.VMEM)] * 4,
         scratch_shapes=[
-            pltpu.VMEM((rows, pieces, capacity, lane), x.dtype),
             pltpu.SMEM(counts.shape, counts.dtype),
             pltpu.SMEM(frequency.shape, frequency.dtype),
             pltpu.VMEM(val_band.shape, val_band.dtype),
@@ -639,6 +818,13 @@
             dma((rows,)),
             dma((rows,)),
             dma((rows, half + 1)),
+            pltpu.VMEM((half, capacity, lane), x.dtype),
+            dma(()),
+            dma((half,)),
+            dma(()),
+            dma((half, 2)),
+            dma(()),
+            dma(()),
         ],
         compiler_params=pltpu.CompilerParams(
             collective_id=0, has_side_effects=True, vmem_limit_bytes=VMEM - room - SPARE
@@ -646,59 +832,77 @@
     )(x, counts, frequency, val_band, cond_band, val_energy, cond_energy)
 
 
-def stream_kernel(weights, choose_ref, seg_ref, packed_ref, out_ref, turned, buf, sem):
-    freqs, depth = weights.shape[0], choose_ref.shape[0]
+def stream_kernel(weights, choose_ref, seg_ref, cols_ref, out_ref, turned, packed, buf, sem):
+    freqs = weights.shape[0]
     rows, chunks, capacity, lane = seg_ref.shape
-    depth_slots = rows * capacity
-    slots, part = buf.shape[0], buf.shape[2] // sem.shape[1]
-    total = chunks * freqs
-
-    def put(t, n):
-        tall = pl.ds(pl.multiple_of((t // freqs) * lane, lane), lane)
-        return pltpu.make_async_copy(
-            buf.at[t % slots, :, pl.ds(n * part, part)],
-            out_ref.at[t % freqs, tall, pl.ds(n * part, part)],
-            sem.at[t % slots, n],
+    slots, width = rows * capacity, packed.shape[1]
+    firsts, parts = sem.shape[1], PARTS
+    first, part = width // firsts, width // parts
+    group = first // lane
+
+    def put(chunk, f, n, wide):
+        tall = pl.ds(pl.multiple_of(chunk * lane, lane), lane)
+        across = pl.ds(n * wide, wide)
+        return pltpu.make_async_copy(buf.at[f, :, across], out_ref.at[f, tall, across], sem.at[f, n])
+
+    def turn(chunk):
+        turned[...] = lax.dot_general(
+            seg_ref[:, chunk].reshape(slots, lane), choose_ref[...], (((0,), (1,)), ((), ())),
+            preferred_element_type=jnp.float32,
         )
+
+    def scale(f):
+        return (turned[...] * weights[f][:1]).astype(jnp.bfloat16)
+
+    turn(0)
+    for n in range(firsts):
+        across = pl.ds(n * first, first)
+        for p in range(n * group, (n + 1) * group):
+            packed[:, p * lane : (p + 1) * lane] = jnp.dot(
+                choose_ref[...], cols_ref[:, p].reshape(slots, lane), preferred_element_type=jnp.float32
+            ).astype(jnp.bfloat16)
+        for f in range(freqs):
+            buf[f, :, across] = jnp.dot(scale(f), packed[:, across], preferred_element_type=jnp.float32)
+            put(0, f, n, first).start()
 
     def body(t, carry):
         chunk, f = t // freqs, t % freqs
 
         @pl.when(f == 0)
         def _():
-            piece = seg_ref[:, chunk].reshape(depth_slots, lane)
-            turned[...] = lax.dot_general(
-                piece, choose_ref[...], (((0,), (1,)), ((), ())), preferred_element_type=jnp.float32
-            )
-
-        scaled = (turned[...] * weights[f][:1]).astype(jnp.bfloat16)
-        for n in range(sem.shape[1]):
-            @pl.when(t >= slots)
-            def _():
-                put(t - slots, n).wait()
-
-            buf[t % slots, :, n * part : (n + 1) * part] = jnp.dot(
-                scaled, packed_ref[:, n * part : (n + 1) * part], preferred_element_type=jnp.float32
-            )
-            put(t, n).start()
+            turn(chunk)
+
+        scaled = scale(f)
+        for n in range(parts):
+            @pl.when(chunk == 1)
+            def _():
+                for m in range(n * firsts // parts, (n + 1) * firsts // parts):
+                    put(0, f, m, first).wait()
+
+            @pl.when(chunk > 1)
+            def _():
+                put(chunk - 1, f, n, part).wait()
+
+            across = pl.ds(n * part, part)
+            buf[f, :, across] = jnp.dot(scaled, packed[:, across], preferred_element_type=jnp.float32)
+            put(chunk, f, n, part).start()
 
         return carry
 
-    lax.fori_loop(0, total, body, 0)
-
-    def drain(t, carry):
-        for n in range(sem.shape[1]):
-            put(t, n).wait()
+    lax.fori_loop(freqs, chunks * freqs, body, 0)
+
+    def drain(f, carry):
+        for n in range(parts):
+            put(chunks - 1, f, n, part).wait()
         return carry
 
-    lax.fori_loop(max(total - slots, 0), total, drain, 0)
-
-
-def stream_product(weights, choose, seg, packed):
+    lax.fori_loop(0, freqs, drain, 0)
+
+
+def stream_product(weights, choose, seg, columns):
     freqs = weights.shape[0]
     rows, chunks, capacity, lane = seg.shape
-    depth, width = packed.shape
-    parts = PARTS
+    width, depth = columns.shape[1] * lane, choose.shape[0]
     vmem = pl.BlockSpec(memory_space=pltpu.VMEM)
     return pl.pallas_call(
         stream_kernel,
@@ -707,20 +911,21 @@
         out_specs=pl.BlockSpec(memory_space=pl.ANY),
         scratch_shapes=[
             pltpu.VMEM((lane, depth), jnp.float32),
-            pltpu.VMEM((BUFFERS, lane, width), jnp.float32),
-            pltpu.SemaphoreType.DMA((BUFFERS, parts)),
+            pltpu.VMEM((depth, width), jnp.bfloat16),
+            pltpu.VMEM((freqs, lane, width), jnp.float32),
+            pltpu.SemaphoreType.DMA((freqs, FIRST_PARTS)),
         ],
         compiler_params=pltpu.CompilerParams(vmem_limit_bytes=40 * 1024 * 1024),
-    )(weights, choose, seg, packed)
+    )(weights, choose, seg, columns)
 
 
 def per_device(pair_elems, counts, val_band, cond_band, val_energy, cond_energy, frequency):
     rows, cols = lax.axis_size("row"), lax.axis_size("col")
     if cols == 4 and rows == 2 * cols and pair_elems.shape[1] % (128 * PIECES) == 0:
-        packed, seg, choose, weights = plane_gather(
+        columns, seg, choose, weights = plane_gather(
             pair_elems, counts, frequency, val_band, cond_band, val_energy, cond_energy, rows, cols
         )
-        return stream_product(weights, choose, seg, packed)
+        return stream_product(weights, choose, seg, columns)
     columns, seg, choose, weights = gather(
         pair_elems, counts, frequency, val_band, cond_band, val_energy, cond_energy, rows, cols
     )

time: 47 us -> 44 us (0.936)
  the two profiles are of different devices: /device:TPU:25 before, /device:TPU:3 now
where the time goes in v3:
time: 44 us; the launch traced here: 43.2 us
  Pallas kernels  43.2 us (98%)
    pallas_call x1, Pallas kernels, plane_gather(): pl.pallas_call(functools.partial(plane_gather_kernel, rows, cols), out_sh...  24.3 us
    pallas_call x1, Pallas kernels, stream_product(): pl.pallas_call(stream_kernel, out_shape=jax.ShapeDtypeStruct((freqs, chun...  18.8 us

profile of v3, /device:TPU:3, one launch (start us, length us, event | category | flops | bytes accessed | tf_op | source)
XLA Modules:
  0.0 43.2 jit_solution(14922171776059194951)
XLA Ops:
  0.0 24.3 %shard_map.73 = (bf16[8,8,40,384]{3,2,1,0:T(8,128)(2,1)S(1)}, bf16[8,4,40,384]{3,2,1,0:T(8,128)(2,1)S(1)}, bf16[256,320]{1,0:T(8,128)(2,1)S(1)}, f32[3,8,256]{2,1,0:T(8,128)S(1)}) custom-call(bf16[40,3072]{1,0:T(8,128)(2,1)} %x_ref.1, s32[8]{0:T(128)} %counts_hbm.1, f32[3]{0:T(128)} %freq_hbm.1, s32[320]{0:T(512)} %val_band_hbm.1, s32[320]{0:T(512)} %cond_band_hbm.1, ...), custom_call_target="tpu_custom_call" | custom-call | tf_op jit(solution)/shard_map/pallas_call | solution.py:795
  24.4 18.8 %shard_map.74 = f32[3,1536,3072]{2,1,0:T(8,128)} custom-call(f32[3,8,256]{2,1,0:T(8,128)S(1)} %get-tuple-element.9.weights, bf16[256,320]{1,0:T(8,128)(2,1)S(1)} %get-tuple-element.10.choose_ref, bf16[8,4,40,384]{3,2,1,0:T(8,128)(2,1)S(1)} %get-tuple-element.11.seg_ref, bf16[8,8,40,384]{3,2,1,0:T(8,128)(2,1)S(1)} %get-tuple-element.12.cols_ref), custom_call_target="tpu_custom_call" | custom-call | tf_op jit(solution)/shard_map/pallas_call | solution.py:907

commit v4 on v3

--- a/solution.py
+++ b/solution.py
@@ -16,9 +16,9 @@
 PIECES = 8
 PARTS = 2
 FIRST_PARTS = 4
-ROLE_DELAYS = {True: {False: (3, -1), True: (6, 2)}, False: {False: (8, 8), True: (16, 16)}}
-HOLD_STEP = 3
-SPREAD_STEP = 11
+ROLE_DELAYS = {True: {False: (3, 0), True: (6, 3)}, False: {False: (7, 7), True: (14, 14)}}
+HOLD_STEP = 0
+SPREAD_STEP = 10
 
 
 def ring_place(c, count):
@@ -359,7 +359,7 @@
 def plane_gather_kernel(rows, cols, x_ref, counts_hbm, freq_hbm, val_band_hbm, cond_band_hbm, val_energy_hbm,
                         cond_energy_hbm, cols_ref, seg_ref, choose_ref, weights_ref, counts_ref, freq_ref,
                         val_band, cond_band, val_energy, cond_energy, small_sem, own_sem, line_send, line_recv, mate_send,
-                        mate_recv, enter_send, relay_send, seg_recv, held, held_send, held_recv, aid_send,
+                        mate_recv, enter_send, relay_send, seg_recv, held, held_send, held_recv, direct_send, aid_send,
                         aid_recv, aid_mate_send, aid_mate_recv):
     r, c = lax.axis_index("row"), lax.axis_index("col")
     chips = rows // 2
@@ -401,35 +401,41 @@
         pl.semaphore_signal(barrier, inc=1, device_id=(row, col), device_id_type=MESH)
 
     mate = 2 * q + 1 - k
-    greet(mate, c)
-    for turn in range(1, cols):
-        greet(r, chip_at(place + turn))
+    across = end | (target_rel % 2 == 0) | (rel % 2 == 0)
+
+    @pl.when(across)
+    def _():
+        greet(r, chip_at(place + 2))
+
+    crossing = (end & (rel >= 2)) | (helper & (target_rel >= 2))
+
+    @pl.when(crossing)
+    def _():
+        greet(2 * jnp.where(end, beside, target) + 1 - k, c)
+
+    @pl.when(up_ok)
+    def _():
+        greet(r + 2, c)
+
+    @pl.when(down_ok)
+    def _():
+        greet(r - 2, c)
 
     @pl.when(is_source)
     def _():
         greet(mate, near[0])
         greet(mate, near[1])
-
-    @pl.when(rel % 2 == 1)
+        greet(mate, chip_at(place + 2))
+
+    @pl.when(~is_source)
     def _():
         greet(mate, chip_at(place - rel))
 
-    @pl.when(up_ok)
-    def _():
-        greet(r + 2, c)
-
-    @pl.when(down_ok)
-    def _():
-        greet(r - 2, c)
-
-    crossing = (end & ~is_source) | (helper & (target_rel != 0))
-
-    @pl.when(crossing)
-    def _():
-        greet(2 * jnp.where(end, beside, target) + 1 - k, c)
-
-    calls = cols + jnp.where(is_source, 2, rel % 2) + (up_ok.astype(jnp.int32) + down_ok.astype(jnp.int32))
-    pl.semaphore_wait(barrier, calls + crossing.astype(jnp.int32))
+    greet(r, near[0])
+    greet(r, near[1])
+    greet(mate, c)
+    calls = 3 + jnp.where(is_source, 3, 1) + up_ok.astype(jnp.int32) + down_ok.astype(jnp.int32)
+    pl.semaphore_wait(barrier, calls + across.astype(jnp.int32) + crossing.astype(jnp.int32))
     for copy in own:
         copy.wait()
 
@@ -460,6 +466,10 @@
     def enter_copy(b, p, way):
         arrival = seg_recv.at[b, jnp.where(p % 2 == way, p % half, half)]
         return remote(cols_ref.at[b, p], seg_ref.at[b, p % half], enter_send.at[b], arrival, 2 * q + p // half, near[way])
+
+    def direct_copy(b, p):
+        arrival = seg_recv.at[b, half]
+        return remote(cols_ref.at[b, p], seg_ref.at[b, p % half], direct_send, arrival, 2 * q + p // half, chip_at(place + 2))
 
     def relay_copy(d, b, p, way):
         last = (rel == 2) | tree(d)
@@ -518,9 +528,15 @@
             toward = target > q if stream == 0 else target < q
             spared = helper & (target_rel == 0) & toward & (p % half >= half // 2)
 
-            @pl.when(onward(stream) & ~spared)
+            paired = helper & (target_rel != 0) & toward
+
+            @pl.when(onward(stream) & ~spared & ~paired)
             def _():
                 line_copy(stream, 0, cols_ref.at[r, p], line_recv.at[stream, 0, p]).start()
+
+            @pl.when(onward(stream) & paired & (p % 2 == 1))
+            def _():
+                line_copy(stream, 0, cols_ref.at[r, pl.ds(p - 1, 2)], line_recv.at[stream, 0, p]).start()
 
         feed(0, p, r)
         mate_copy(r, cols_ref.at[r, p]).start()
@@ -583,22 +599,37 @@
                 (0, 2 * (q - d) + k, r + 2, (d > 0) & (d <= q)),
                 (1, 2 * (q + d) + k, r - 2, (d > 0) & (d < chips - q)),
             ]
+        paired = ends and not source
+        if paired and p % 2 == 0:
+            return
         for stream, b, row, present in streams:
             if ends and source and p % half >= half // 2:
                 present = present & (d > 1)
 
             @pl.when(present)
             def _():
-                piece = cols_ref.at[b, p]
+                piece = cols_ref.at[b, pl.ds(p - 1, 2)] if paired else cols_ref.at[b, p]
                 await_arrivals(piece, line_recv.at[stream, d - 1, p])
                 if row is not None:
-                    remote(piece, piece, line_send.at[stream, d], line_recv.at[stream, d, p], row, c).start()
+                    double = (target_rel != 0) & ((target > q) if stream == 0 else (target < q))
+
+                    @pl.when(~double)
+                    def _():
+                        line_copy(stream, d, piece, line_recv.at[stream, d, p]).start()
+
+                    if p % 2 == 1:
+                        @pl.when(double)
+                        def _():
+                            line_copy(stream, d, cols_ref.at[b, pl.ds(p - 1, 2)], line_recv.at[stream, d, p]).start()
+
                 if source:
-                    enter_copy(b, p, p % 2).start()
-
                     @pl.when(tree(d))
                     def _():
+                        if p == pieces - 1:
+                            direct_copy(b, p).start()
                         enter_copy(b, p, 1 - p % 2).start()
+
+                    enter_copy(b, p, p % 2).start()
 
                 mate_copy(b, piece).start()
 
@@ -623,7 +654,10 @@
                     for core in (0, 1):
                         b = first + core
                         await_arrivals(seg_ref.at[b, p % half], seg_recv.at[b, p % half])
-                        relay_copy(d, b, p, p % 2).start()
+
+                        @pl.when(~tree(d) | (p < pieces - 1))
+                        def _():
+                            relay_copy(d, b, p, p % 2).start()
 
     def role(ends, place_in_ring):
         source, opposite = place_in_ring == 0, place_in_ring == 2
@@ -724,6 +758,7 @@
                 @pl.when(is_source & tree(d))
                 def _():
                     await_sends(cols_ref.at[pl.ds(0, 2)], enter_send.at[b])
+                    await_sends(cols_ref.at[b, 0], direct_send)
 
                 @pl.when(is_source & ~tree(d) & ~part)
                 def _():
@@ -734,7 +769,16 @@
                     for some, count in ((part, half // 2), (~part, half)):
                         @pl.when(some & ((rel == 1) | (rel == cols - 1)))
                         def _():
-                            await_sends(seg_ref.at[e, pl.ds(0, count // 2)], relay_send.at[e])
+                            fewer = (rel == cols - 1) & tree(d) & (k == 1)
+
+                            @pl.when(fewer)
+                            def _():
+                                await_sends(seg_ref.at[e, pl.ds(0, max(count // 2 - 1, 1))], relay_send.at[e])
+
+                            @pl.when(~fewer)
+                            def _():
+                                await_sends(seg_ref.at[e, pl.ds(0, count // 2)], relay_send.at[e])
+
                             await_arrivals(seg_ref.at[e, pl.ds(0, count // 2)], seg_recv.at[e, half])
 
                         @pl.when(some & (rel == 2) & ~tree(d))
@@ -822,6 +866,7 @@
             dma(()),
             dma((half,)),
             dma(()),
+            dma(()),
             dma((half, 2)),
             dma(()),
             dma(()),

time: 44 us -> 43.9 us (level)
  no operation moved by 1% of the time
where the time goes in v4:
time: 43.9 us; the launch traced here: 43.1 us
  Pallas kernels  43.1 us (98%)
    pallas_call x1, Pallas kernels, plane_gather(): pl.pallas_call(functools.partial(plane_gather_kernel, rows, cols), out_sh...  24.2 us
    pallas_call x1, Pallas kernels, stream_product(): pl.pallas_call(stream_kernel, out_shape=jax.ShapeDtypeStruct((freqs, chun...  18.8 us

profile of v4, /device:TPU:3, one launch (start us, length us, event | category | flops | bytes accessed | tf_op | source)
XLA Modules:
  0.0 43.1 jit_solution(13468140160856863106)
XLA Ops:
  0.0 24.2 %shard_map.73 = (bf16[8,8,40,384]{3,2,1,0:T(8,128)(2,1)S(1)}, bf16[8,4,40,384]{3,2,1,0:T(8,128)(2,1)S(1)}, bf16[256,320]{1,0:T(8,128)(2,1)S(1)}, f32[3,8,256]{2,1,0:T(8,128)S(1)}) custom-call(bf16[40,3072]{1,0:T(8,128)(2,1)} %x_ref.1, s32[8]{0:T(128)} %counts_hbm.1, f32[3]{0:T(128)} %freq_hbm.1, s32[320]{0:T(512)} %val_band_hbm.1, s32[320]{0:T(512)} %cond_band_hbm.1, ...), custom_call_target="tpu_custom_call" | custom-call | tf_op jit(solution)/shard_map/pallas_call | solution.py:839
  24.2 18.8 %shard_map.74 = f32[3,1536,3072]{2,1,0:T(8,128)} custom-call(f32[3,8,256]{2,1,0:T(8,128)S(1)} %get-tuple-element.9.weights, bf16[256,320]{1,0:T(8,128)(2,1)S(1)} %get-tuple-element.10.choose_ref, bf16[8,4,40,384]{3,2,1,0:T(8,128)(2,1)S(1)} %get-tuple-element.11.seg_ref, bf16[8,8,40,384]{3,2,1,0:T(8,128)(2,1)S(1)} %get-tuple-element.12.cols_ref), custom_call_target="tpu_custom_call" | custom-call | tf_op jit(solution)/shard_map/pallas_call | solution.py:952

commit v5 on v4

--- a/solution.py
+++ b/solution.py
@@ -877,7 +877,7 @@
     )(x, counts, frequency, val_band, cond_band, val_energy, cond_energy)
 
 
-def stream_kernel(weights, choose_ref, seg_ref, cols_ref, out_ref, turned, packed, buf, sem):
+def stream_kernel(weights, choose_ref, seg_ref, cols_ref, out_ref, turned, ready, packed, buf, sem):
     freqs = weights.shape[0]
     rows, chunks, capacity, lane = seg_ref.shape
     slots, width = rows * capacity, packed.shape[1]
@@ -907,7 +907,9 @@
                 choose_ref[...], cols_ref[:, p].reshape(slots, lane), preferred_element_type=jnp.float32
             ).astype(jnp.bfloat16)
         for f in range(freqs):
-            buf[f, :, across] = jnp.dot(scale(f), packed[:, across], preferred_element_type=jnp.float32)
+            if n == 0:
+                ready[f] = scale(f)
+            buf[f, :, across] = jnp.dot(ready[f], packed[:, across], preferred_element_type=jnp.float32)
             put(0, f, n, first).start()
 
     def body(t, carry):
@@ -956,6 +958,7 @@
         out_specs=pl.BlockSpec(memory_space=pl.ANY),
         scratch_shapes=[
             pltpu.VMEM((lane, depth), jnp.float32),
+            pltpu.VMEM((freqs, lane, depth), jnp.bfloat16),
             pltpu.VMEM((depth, width), jnp.bfloat16),
             pltpu.VMEM((freqs, lane, width), jnp.float32),
             pltpu.SemaphoreType.DMA((freqs, FIRST_PARTS)),

time: 43.9 us -> 43.9 us (level)
  no operation moved by 1% of the time
where the time goes in v5:
time: 43.9 us; the launch traced here: 43.1 us
  Pallas kernels  43.1 us (98%)
    pallas_call x1, Pallas kernels, plane_gather(): pl.pallas_call(functools.partial(plane_gather_kernel, rows, cols), out_sh...  24.2 us
    pallas_call x1, Pallas kernels, stream_product(): pl.pallas_call(stream_kernel, out_shape=jax.ShapeDtypeStruct((freqs, chun...  18.8 us

profile of v5, /device:TPU:3, one launch (start us, length us, event | category | flops | bytes accessed | tf_op | source)
XLA Modules:
  0.0 43.1 jit_solution(2857497281390912325)
XLA Ops:
  0.0 24.2 %shard_map.73 = (bf16[8,8,40,384]{3,2,1,0:T(8,128)(2,1)S(1)}, bf16[8,4,40,384]{3,2,1,0:T(8,128)(2,1)S(1)}, bf16[256,320]{1,0:T(8,128)(2,1)S(1)}, f32[3,8,256]{2,1,0:T(8,128)S(1)}) custom-call(bf16[40,3072]{1,0:T(8,128)(2,1)} %x_ref.1, s32[8]{0:T(128)} %counts_hbm.1, f32[3]{0:T(128)} %freq_hbm.1, s32[320]{0:T(512)} %val_band_hbm.1, s32[320]{0:T(512)} %cond_band_hbm.1, ...), custom_call_target="tpu_custom_call" | custom-call | tf_op jit(solution)/shard_map/pallas_call | solution.py:839
  24.2 18.8 %shard_map.74 = f32[3,1536,3072]{2,1,0:T(8,128)} custom-call(f32[3,8,256]{2,1,0:T(8,128)S(1)} %get-tuple-element.9.weights, bf16[256,320]{1,0:T(8,128)(2,1)S(1)} %get-tuple-element.10.choose_ref, bf16[8,4,40,384]{3,2,1,0:T(8,128)(2,1)S(1)} %get-tuple-element.11.seg_ref, bf16[8,8,40,384]{3,2,1,0:T(8,128)(2,1)S(1)} %get-tuple-element.12.cols_ref), custom_call_target="tpu_custom_call" | custom-call | tf_op jit(solution)/shard_map/pallas_call | solution.py:954
